TPU v7x, 256 devices: a whole 4x4x8 slice. The times are simulated.
256 devices in a mesh: gx: 8 (over x, core), gy: 32 (over y, z).
Axes of the slice: x: 4, y: 4, z: 8, core: 2. Of those that a mesh axis runs over, the one named last changes fastest.
Arguments:
- fields: bfloat16 [672, 672, 1536], P('gx', 'gy'), may hold values from -16 to 16
- x_factor: bfloat16 [672, 336], replicated, may hold values from -0.00030517578 to 0.00030517578
- running_r: float32 [672, 672], replicated, as said below
Outputs:
- new_r: float32 [672, 672], P('gy', 'gx')
Inputs may be any that keep to these rules, and one draw needn't show every extreme that they name: `running_r`: upper triangular with a positive diagonal.
All inputs are finite; a program needn't handle non-finite values.
Results may differ from a plain program's by a relative error of at most 0.0003.
Values may be sent and summed in bfloat16 or wider, within the bound.
A program may use at most 256 MiB of HBM per device.

v0:
```python
import jax
import jax.numpy as jnp
from jax import lax
from jax.sharding import PartitionSpec as P


def fibre_gram(fibres):
    local_gram = lax.dot_general(
        fibres, fibres, (((0, 2), (0, 2)), ((), ())), preferred_element_type=jnp.float32
    )
    return lax.psum(local_gram, ("gx", "gy"))


def project_local(x_factor, block):
    full_x = block.shape[0]
    middle = block.shape[1]
    part_cells = block.shape[2]
    product = lax.dot_general(
        x_factor,
        block.reshape(full_x, middle * part_cells),
        (((0,), (0,)), ((), ())),
        preferred_element_type=jnp.float32,
    )
    return product.astype(jnp.bfloat16).reshape(x_factor.shape[1], middle, part_cells)


def on_device(fields, x_factor, running_r):
    full_y = running_r.shape[0]
    exchanged = lax.all_to_all(fields, "gx", split_axis=2, concat_axis=0, tiled=True)
    projected = project_local(x_factor, exchanged)
    fibres = lax.all_to_all(projected, "gy", split_axis=2, concat_axis=1, tiled=True)
    gram_sum = fibre_gram(fibres)
    total = (
        jnp.dot(
            running_r.T,
            running_r,
            precision=lax.Precision.HIGHEST,
            preferred_element_type=jnp.float32,
        )
        + gram_sum
    )
    upper_r = jnp.linalg.cholesky(total).T
    row_block = full_y // lax.axis_size("gy")
    col_block = full_y // lax.axis_size("gx")
    return lax.dynamic_slice(
        upper_r,
        (lax.axis_index("gy") * row_block, lax.axis_index("gx") * col_block),
        (row_block, col_block),
    )


def solution(mesh):
    in_specs = (P("gx", "gy", None), P(), P())
    out_specs = P("gy", "gx")
    return jax.shard_map(
        on_device, mesh=mesh, in_specs=in_specs, out_specs=out_specs, check_vma=False
    )
```

profile of v0, /device:TPU:2, one launch (start us, length us, event | category | flops | bytes accessed | tf_op | source)
XLA Modules:
  0.0 698.8 jit_solution(13633956588699801760)
XLA Ops:
  6.5 0.0 copy-start
  6.5 0.0 all-reduce.3.cloned.1.call-start
  6.5 11.8 %copy.19 = bf16[84,21,1536]{0,1,2:T(8,128)(2,1)} copy(bf16[84,21,1536]{2,0,1:T(8,128)(2,1)} %param.3) | data formatting | bytes 10838016 | tf_op args[0]
  18.4 114.1 %all_to_all.33 = bf16[84,21,1536]{0,1,2:T(8,128)(2,1)} all-to-all(bf16[84,21,1536]{0,1,2:T(8,128)(2,1)} %copy.19), channel_id=1, replica_groups=mesh['gx'=8,'gy'=32] {'gx'}, dimensions={2} | all-to-all | bytes 10838016 | tf_op jit(solution)/shard_map/all_to_all | solution.py:29
  132.5 15.4 %copy.20 = bf16[84,21,8,192]{3,1,0,2:T(8,128)(2,1)} copy(bf16[84,21,8,192]{0,1,3,2:T(8,128)(2,1)} %bitcast.50) | data formatting | bytes 10838016 | tf_op jit(solution)/shard_map/all_to_all | solution.py:29
  147.9 0.0 copy-start.2
  147.9 12.5 %reshape.46 = bf16[672,4032]{1,0:T(8,128)(2,1)} reshape(bf16[8,84,21,192]{3,2,1,0:T(8,128)(2,1)} %bitcast.51) | data formatting | bytes 10838016 | tf_op jit(solution)/shard_map/reshape | solution.py:20
  160.4 0.0 copy-done.2
  160.4 6.4 convolution_convert_fusion
  166.8 4.5 copy.21
  171.3 3.7 copy.22
  175.1 91.4 %all_to_all.34 = bf16[336,21,192]{0,1,2:T(8,128)(2,1)S(1)} all-to-all(bf16[336,21,192]{0,1,2:T(8,128)(2,1)S(1)} %copy.22), channel_id=1, replica_groups=mesh['gx'=8,'gy'=32] {'gy'}, dimensions={2} | all-to-all | bytes 5419008 | tf_op jit(solution)/shard_map/all_to_all | solution.py:31
  266.5 2.2 copy.23
  268.7 6.0 all_to_all.30
  274.7 6.8 convolution_bitcast_fusion
  281.5 0.0 all-reduce.3.cloned.1.call-update
  281.5 257.3 %all-reduce.3.cloned.1.call-done = f32[672,672]{0,1:T(8,128)} async-done(((f32[672,672]{0,1:T(8,128)}), f32[672,672]{0,1:T(8,128)}) %all-reduce.3.cloned.1.call-update) | async-done | bytes 1806352 | tf_op jit(solution)/shard_map/psum | solution.py:11
  538.8 0.0 copy-done
  538.8 8.2 %convolution_add_fusion = f32[672,672]{0,1:T(8,128)} fusion(f32[672,672]{0,1:T(8,128)} %all-reduce.3.cloned.1.call-done, f32[672,672]{1,0:T(8,128)S(1)} %copy-done), kind=kOutput, calls=%fused_computation.4 | convolution fusion | flops 3642024960 | bytes 5419008 | tf_op jit(solution)/shard_map/dot_general | solution.py:34
  547.0 3.1 copy.27
  550.2 2.5 fusion
  552.6 0.0 copy-start.1
  552.7 1.3 copy-done.1
  554.0 11.7 %cholesky.166 = f32[128,128]{1,0:T(8,128)S(1)} custom-call(f32[128,128]{1,0:T(8,128)S(1)} %cholesky.430), custom_call_target="Cholesky" | custom-call | tf_op jit(solution)/shard_map/jit(cholesky)/cholesky | solution.py:42
  565.7 9.8 %custom-call.43 = f32[1,128,128]{1,2,0:T(8,128)S(1)} custom-call(f32[1,128,128]{2,1,0:T(8,128)S(1)} %get-tuple-element.18), custom_call_target="InvertDiagBlocksLowerTriangular" | custom-call | tf_op jit(solution)/shard_map/jit(cholesky)/cholesky | solution.py:42
  575.6 1.4 cholesky.342
  577.0 2.1 constant_dynamic-update-slice_fusion.4
  579.0 1.3 convolution_subtract_fusion
  580.4 11.7 %cholesky.189 = f32[128,128]{1,0:T(8,128)S(1)} custom-call(f32[128,128]{1,0:T(8,128)S(1)} %cholesky.434), custom_call_target="Cholesky" | custom-call | tf_op jit(solution)/shard_map/jit(cholesky)/cholesky | solution.py:42
  592.1 0.7 select_reduce_fusion.3
  592.8 10.2 %custom-call.44 = f32[1,128,128]{1,2,0:T(8,128)S(1)} custom-call(f32[1,128,128]{2,1,0:T(8,128)S(1)} %get-tuple-element.15), custom_call_target="InvertDiagBlocksLowerTriangular" | custom-call | tf_op jit(solution)/shard_map/jit(cholesky)/cholesky | solution.py:42
  603.0 1.0 convolution_dynamic-update-slice_fusion
  604.0 1.6 convolution_subtract_fusion.1
  605.6 11.7 %cholesky.356 = f32[128,128]{1,0:T(8,128)S(1)} custom-call(f32[128,128]{1,0:T(8,128)S(1)} %cholesky.439), custom_call_target="Cholesky" | custom-call | tf_op jit(solution)/shard_map/jit(cholesky)/cholesky | solution.py:42
  617.3 0.6 select_reduce_fusion.2
  618.0 0.7 compare_reduce_fusion.3
  618.7 9.8 %custom-call.45 = f32[1,128,128]{1,2,0:T(8,128)S(1)} custom-call(f32[1,128,128]{2,1,0:T(8,128)S(1)} %get-tuple-element.12), custom_call_target="InvertDiagBlocksLowerTriangular" | custom-call | tf_op jit(solution)/shard_map/jit(cholesky)/cholesky | solution.py:42
  628.5 1.0 convolution_dynamic-update-slice_fusion.1
  629.4 1.7 convolution_subtract_fusion.2
  631.1 11.8 %cholesky.375 = f32[128,128]{1,0:T(8,128)S(1)} custom-call(f32[128,128]{1,0:T(8,128)S(1)} %cholesky.444), custom_call_target="Cholesky" | custom-call | tf_op jit(solution)/shard_map/jit(cholesky)/cholesky | solution.py:42
  643.0 0.6 select_reduce_fusion.1
  643.6 0.7 compare_reduce_fusion.2
  644.3 9.8 %custom-call.46 = f32[1,128,128]{1,2,0:T(8,128)S(1)} custom-call(f32[1,128,128]{2,1,0:T(8,128)S(1)} %get-tuple-element.9), custom_call_target="InvertDiagBlocksLowerTriangular" | custom-call | tf_op jit(solution)/shard_map/jit(cholesky)/cholesky | solution.py:42
  654.1 0.9 convolution_dynamic-update-slice_fusion.2
  655.0 1.5 convolution_subtract_fusion.3
  656.5 11.7 %cholesky.394 = f32[128,128]{1,0:T(8,128)S(1)} custom-call(f32[128,128]{1,0:T(8,128)S(1)} %cholesky.449), custom_call_target="Cholesky" | custom-call | tf_op jit(solution)/shard_map/jit(cholesky)/cholesky | solution.py:42
  668.2 0.6 select_reduce_fusion
  668.9 0.7 compare_reduce_fusion.1
  669.5 9.8 %custom-call.47 = f32[1,128,128]{1,2,0:T(8,128)S(1)} custom-call(f32[1,128,128]{2,1,0:T(8,128)S(1)} %get-tuple-element.6), custom_call_target="InvertDiagBlocksLowerTriangular" | custom-call | tf_op jit(solution)/shard_map/jit(cholesky)/cholesky | solution.py:42
  679.3 0.8 convolution_dynamic-update-slice_fusion.3
  680.1 1.2 convolution_subtract_fusion.4
  681.3 2.9 cholesky.415
  684.2 0.6 select_reduce_fusion.5
  684.8 0.7 compare_reduce_fusion
  685.6 0.6 compare_reduce_fusion.4
  690.0 1.0 fusion.20
  691.0 0.7 copy.28
  (6 shorter events, 0.1 us)
Async XLA Ops:
  6.5 532.3 %copy-start = (f32[672,672]{1,0:T(8,128)S(1)}, f32[672,672]{1,0:T(8,128)}, u32[]{:S(2)}) copy-start(f32[672,672]{1,0:T(8,128)} %param.5) | copy-start | bytes 5419012
  6.5 532.3 %all-reduce.3.cloned.1.call-start = ((), (), s32[]{:S(2)}) async-start(), calls=%async_computation.2 | async-start | bytes 4128768 | tf_op jit(solution)/shard_map/psum | solution.py:11
  147.9 12.5 %copy-start.2 = (bf16[672,336]{1,0:T(8,128)(2,1)S(1)}, bf16[672,336]{1,0:T(8,128)(2,1)}, u32[]{:S(2)}) copy-start(bf16[672,336]{1,0:T(8,128)(2,1)} %param.4) | copy-start | bytes 1354756
  552.6 1.3 copy-start.1
Sparse Core Ops, SparseCore 0:
  281.6 257.1 all-reduce.2
where the time goes:
time: 706 us; the launch traced here: 699 us
  waiting for transfers between devices  257 us (36%)
  blocking collectives  206 us (29%)
  other arithmetic  121 us (17%)
  local copies, waits for them, and re-layouts  62.8 us (9%)
  matrix products  34.5 us (5%)
  between operations  17.6 us (2%)
    psum x1, waiting for transfers between devices, fibre_gram(): return lax.psum(local_gram, ('gx', 'gy'))  257 us
    another operation x22, other arithmetic, on_device(): upper_r = jnp.linalg.cholesky(total).T  118 us
    all_to_all x1, blocking collectives, on_device(): lax.all_to_all(fields, 'gx', split_axis=2, concat_axis=0, tiled=True)  114 us
    all_to_all x1, blocking collectives, on_device(): lax.all_to_all(projected, 'gy', split_axis=2, concat_axis=1, tiled=True)  91.4 us
    all_to_all x1, local copies, waits for them, and re-layouts, on_device(): lax.all_to_all(fields, 'gx', split_axis=2, concat_axis=0, tiled=True)  15.4 us
  transfers between devices with their start and end apart: 1, of which 1 were waited for; matrix products, arithmetic and copies ran while one was open for 0% of the time, Pallas kernels for 0%

commit v1 on v0

--- a/solution.py
+++ b/solution.py
@@ -8,7 +8,7 @@
     local_gram = lax.dot_general(
         fibres, fibres, (((0, 2), (0, 2)), ((), ())), preferred_element_type=jnp.float32
     )
-    return lax.psum(local_gram, ("gx", "gy"))
+    return lax.psum(lax.psum(local_gram, "gy"), "gx")
 
 
 def project_local(x_factor, block):

time: 706 us -> 669 us (0.948)
  waiting for transfers between devices: 257 us -> 217 us
    psum x1 -> x2, waiting for transfers between devices: 257 us -> 217 us  [fibre_gram(): return lax.psum(lax.psum(local_gram, 'gy'), 'gx')]
  transfers between devices with their start and end apart: 1 -> 2, of which waited for: 1 -> 2; matrix products, arithmetic and copies ran while one was open for 0% -> 0% of each run, Pallas kernels for 0% -> 0%
where the time goes in v1:
time: 669 us; the launch traced here: 659 us
  waiting for transfers between devices  217 us (32%)
  blocking collectives  205 us (31%)
  other arithmetic  121 us (18%)
  local copies, waits for them, and re-layouts  62.7 us (9%)
  matrix products  34.5 us (5%)
  between operations  17.6 us (3%)
    psum x2, waiting for transfers between devices, fibre_gram(): return lax.psum(lax.psum(local_gram, 'gy'), 'gx')  217 us
    another operation x22, other arithmetic, on_device(): upper_r = jnp.linalg.cholesky(total).T  118 us
    all_to_all x1, blocking collectives, on_device(): lax.all_to_all(fields, 'gx', split_axis=2, concat_axis=0, tiled=True)  114 us
    all_to_all x1, blocking collectives, on_device(): lax.all_to_all(projected, 'gy', split_axis=2, concat_axis=1, tiled=True)  91.2 us
    all_to_all x1, local copies, waits for them, and re-layouts, on_device(): lax.all_to_all(fields, 'gx', split_axis=2, concat_axis=0, tiled=True)  15.4 us
  transfers between devices with their start and end apart: 2, of which 2 were waited for; matrix products, arithmetic and copies ran while one was open for 0% of the time, Pallas kernels for 0%

profile of v1, /device:TPU:2, one launch (start us, length us, event | category | flops | bytes accessed | tf_op | source)
XLA Modules:
  0.0 658.6 jit_solution(6730911013338022619)
XLA Ops:
  6.5 0.0 copy-start
  6.5 0.0 all-reduce.4.cloned.1.call-start
  6.5 11.8 %copy.19 = bf16[84,21,1536]{0,1,2:T(8,128)(2,1)} copy(bf16[84,21,1536]{2,0,1:T(8,128)(2,1)} %param.3) | data formatting | bytes 10838016 | tf_op args[0]
  18.4 114.1 %all_to_all.33 = bf16[84,21,1536]{0,1,2:T(8,128)(2,1)} all-to-all(bf16[84,21,1536]{0,1,2:T(8,128)(2,1)} %copy.19), channel_id=1, replica_groups=mesh['gx'=8,'gy'=32] {'gx'}, dimensions={2} | all-to-all | bytes 10838016 | tf_op jit(solution)/shard_map/all_to_all | solution.py:29
  132.5 15.4 %copy.20 = bf16[84,21,8,192]{3,1,0,2:T(8,128)(2,1)} copy(bf16[84,21,8,192]{0,1,3,2:T(8,128)(2,1)} %bitcast.50) | data formatting | bytes 10838016 | tf_op jit(solution)/shard_map/all_to_all | solution.py:29
  147.9 0.0 copy-start.2
  147.9 12.5 %reshape.46 = bf16[672,4032]{1,0:T(8,128)(2,1)} reshape(bf16[8,84,21,192]{3,2,1,0:T(8,128)(2,1)} %bitcast.51) | data formatting | bytes 10838016 | tf_op jit(solution)/shard_map/reshape | solution.py:20
  160.4 0.0 copy-done.2
  160.4 6.4 convolution_convert_fusion
  166.8 4.5 copy.21
  171.3 3.7 copy.22
  175.1 91.2 %all_to_all.34 = bf16[336,21,192]{0,1,2:T(8,128)(2,1)S(1)} all-to-all(bf16[336,21,192]{0,1,2:T(8,128)(2,1)S(1)} %copy.22), channel_id=1, replica_groups=mesh['gx'=8,'gy'=32] {'gy'}, dimensions={2} | all-to-all | bytes 5419008 | tf_op jit(solution)/shard_map/all_to_all | solution.py:31
  266.3 2.2 copy.23
  268.5 6.0 all_to_all.30
  274.5 6.8 %convolution_bitcast_fusion = f32[672,672]{0,1:T(8,128)} fusion(bf16[336,672,6]{0,1,2:T(8,128)(2,1)} %all_to_all.30), kind=kOutput, calls=%fused_computation.3 | convolution fusion | flops 1820786688 | bytes 4515840 | tf_op jit(solution)/shard_map/dot_general | solution.py:8
  281.3 0.0 all-reduce.4.cloned.1.call-update
  281.3 0.2 all-reduce.6.cloned.1.call-start
  281.6 148.9 %all-reduce.4.cloned.1.call-done = f32[672,672]{0,1:T(8,128)} async-done(((f32[672,672]{0,1:T(8,128)}), f32[672,672]{0,1:T(8,128)}) %all-reduce.4.cloned.1.call-update) | async-done | bytes 1806352 | tf_op jit(solution)/shard_map/psum | solution.py:11
  430.5 0.0 all-reduce.6.cloned.1.call-update
  430.5 68.2 %all-reduce.6.cloned.1.call-done = f32[672,672]{0,1:T(8,128)} async-done(((f32[672,672]{0,1:T(8,128)}), f32[672,672]{0,1:T(8,128)}) %all-reduce.6.cloned.1.call-update) | async-done | bytes 1806352 | tf_op jit(solution)/shard_map/psum | solution.py:11
  498.7 0.0 copy-done
  498.7 8.3 %convolution_add_fusion = f32[672,672]{0,1:T(8,128)} fusion(f32[672,672]{0,1:T(8,128)} %all-reduce.6.cloned.1.call-done, f32[672,672]{1,0:T(8,128)S(1)} %copy-done), kind=kOutput, calls=%fused_computation.4 | convolution fusion | flops 3642024960 | bytes 5419008 | tf_op jit(solution)/shard_map/dot_general | solution.py:34
  507.0 3.1 copy.27
  510.1 2.5 fusion
  512.6 0.0 copy-start.1
  512.6 1.3 copy-done.1
  513.9 11.7 %cholesky.166 = f32[128,128]{1,0:T(8,128)S(1)} custom-call(f32[128,128]{1,0:T(8,128)S(1)} %cholesky.430), custom_call_target="Cholesky" | custom-call | tf_op jit(solution)/shard_map/jit(cholesky)/cholesky | solution.py:42
  525.6 9.8 %custom-call.43 = f32[1,128,128]{1,2,0:T(8,128)S(1)} custom-call(f32[1,128,128]{2,1,0:T(8,128)S(1)} %get-tuple-element.18), custom_call_target="InvertDiagBlocksLowerTriangular" | custom-call | tf_op jit(solution)/shard_map/jit(cholesky)/cholesky | solution.py:42
  535.5 1.4 cholesky.342
  536.9 2.1 constant_dynamic-update-slice_fusion.4
  538.9 1.3 convolution_subtract_fusion
  540.3 11.7 %cholesky.189 = f32[128,128]{1,0:T(8,128)S(1)} custom-call(f32[128,128]{1,0:T(8,128)S(1)} %cholesky.434), custom_call_target="Cholesky" | custom-call | tf_op jit(solution)/shard_map/jit(cholesky)/cholesky | solution.py:42
  552.0 0.7 select_reduce_fusion.3
  552.7 10.2 %custom-call.44 = f32[1,128,128]{1,2,0:T(8,128)S(1)} custom-call(f32[1,128,128]{2,1,0:T(8,128)S(1)} %get-tuple-element.15), custom_call_target="InvertDiagBlocksLowerTriangular" | custom-call | tf_op jit(solution)/shard_map/jit(cholesky)/cholesky | solution.py:42
  562.9 1.0 convolution_dynamic-update-slice_fusion
  563.9 1.6 convolution_subtract_fusion.1
  565.5 11.7 %cholesky.356 = f32[128,128]{1,0:T(8,128)S(1)} custom-call(f32[128,128]{1,0:T(8,128)S(1)} %cholesky.439), custom_call_target="Cholesky" | custom-call | tf_op jit(solution)/shard_map/jit(cholesky)/cholesky | solution.py:42
  577.2 0.6 select_reduce_fusion.2
  577.9 0.7 compare_reduce_fusion.3
  578.6 9.8 %custom-call.45 = f32[1,128,128]{1,2,0:T(8,128)S(1)} custom-call(f32[1,128,128]{2,1,0:T(8,128)S(1)} %get-tuple-element.12), custom_call_target="InvertDiagBlocksLowerTriangular" | custom-call | tf_op jit(solution)/shard_map/jit(cholesky)/cholesky | solution.py:42
  588.4 0.9 convolution_dynamic-update-slice_fusion.1
  589.3 1.7 convolution_subtract_fusion.2
  591.0 11.8 %cholesky.375 = f32[128,128]{1,0:T(8,128)S(1)} custom-call(f32[128,128]{1,0:T(8,128)S(1)} %cholesky.444), custom_call_target="Cholesky" | custom-call | tf_op jit(solution)/shard_map/jit(cholesky)/cholesky | solution.py:42
  602.9 0.6 select_reduce_fusion.1
  603.5 0.7 compare_reduce_fusion.2
  604.2 9.8 %custom-call.46 = f32[1,128,128]{1,2,0:T(8,128)S(1)} custom-call(f32[1,128,128]{2,1,0:T(8,128)S(1)} %get-tuple-element.9), custom_call_target="InvertDiagBlocksLowerTriangular" | custom-call | tf_op jit(solution)/shard_map/jit(cholesky)/cholesky | solution.py:42
  614.0 0.9 convolution_dynamic-update-slice_fusion.2
  614.9 1.5 convolution_subtract_fusion.3
  616.4 11.7 %cholesky.394 = f32[128,128]{1,0:T(8,128)S(1)} custom-call(f32[128,128]{1,0:T(8,128)S(1)} %cholesky.449), custom_call_target="Cholesky" | custom-call | tf_op jit(solution)/shard_map/jit(cholesky)/cholesky | solution.py:42
  628.1 0.6 select_reduce_fusion
  628.8 0.7 compare_reduce_fusion.1
  629.4 9.8 %custom-call.47 = f32[1,128,128]{1,2,0:T(8,128)S(1)} custom-call(f32[1,128,128]{2,1,0:T(8,128)S(1)} %get-tuple-element.6), custom_call_target="InvertDiagBlocksLowerTriangular" | custom-call | tf_op jit(solution)/shard_map/jit(cholesky)/cholesky | solution.py:42
  639.2 0.8 convolution_dynamic-update-slice_fusion.3
  640.0 1.2 convolution_subtract_fusion.4
  641.2 2.9 cholesky.415
  644.1 0.6 select_reduce_fusion.5
  644.7 0.7 compare_reduce_fusion
  645.4 0.6 compare_reduce_fusion.4
  649.9 1.0 fusion.20
  650.9 0.7 copy.28
  (6 shorter events, 0.1 us)
Async XLA Ops:
  6.5 492.2 %copy-start = (f32[672,672]{1,0:T(8,128)S(1)}, f32[672,672]{1,0:T(8,128)}, u32[]{:S(2)}) copy-start(f32[672,672]{1,0:T(8,128)} %param.5) | copy-start | bytes 5419012
  6.5 423.9 %all-reduce.4.cloned.1.call-start = ((), (), s32[]{:S(2)}) async-start(), calls=%async_computation.2 | async-start | bytes 4128768 | tf_op jit(solution)/shard_map/psum | solution.py:11
  147.9 12.5 %copy-start.2 = (bf16[672,336]{1,0:T(8,128)(2,1)S(1)}, bf16[672,336]{1,0:T(8,128)(2,1)}, u32[]{:S(2)}) copy-start(bf16[672,336]{1,0:T(8,128)(2,1)} %param.4) | copy-start | bytes 1354756
  281.3 217.4 %all-reduce.6.cloned.1.call-start = ((), (), s32[]{:S(2)}) async-start(), calls=%async_computation.3 | async-start | bytes 4128768 | tf_op jit(solution)/shard_map/psum | solution.py:11
  512.6 1.3 copy-start.1
Sparse Core Ops, SparseCore 0:
  281.5 148.9 all-reduce.3
  432.8 65.8 all-reduce.5
